TPU v7x, 128 devices: a whole 4x4x4 slice. The times are simulated.
128 devices in a mesh: col: 8 (over z, core), ang: 16 (over y, x).
Axes of the slice: x: 4, y: 4, z: 4, core: 2. Of those that a mesh axis runs over, the one named last changes fastest.
Arguments:
- projections: bfloat16 [128, 256, 8192], P('ang', None, 'col'), may hold values from -8 to 24
- detector_offset: float32 [256, 8192], P(None, 'col'), may hold values from -12 to 12
- drift_offsets: int32 [2, 128], replicated, may hold values from -4 to 4
- drift_fractions: int32 [2, 128], replicated, may hold values from 0 to 255
- cycle_widths: int32 [256], P('ang'), may hold values from 1 to 16
Outputs:
- filtered: float32 [128, 256, 8192], P(None, 'ang', 'col')
Inputs may be any that keep to these rules, and one draw needn't show every extreme that they name: `drift_offsets`: both rows reach -4 and 4.
All inputs are finite; a program needn't handle non-finite values.
Results may differ from a plain program's by a relative error of at most 0.003.
The roundings to bfloat16 on the way count: a program that leaves them out, or rounds other values in their place, can miss the bound.
Values may be sent and summed in bfloat16 or wider, within the bound.
A program may use at most 128 MiB of HBM per device.

v0:
```python
import functools
import math

import jax
import jax.numpy as jnp
from jax import lax
from jax.experimental import pallas as pl
from jax.experimental.pallas import tpu as pltpu
from jax.sharding import PartitionSpec as P

BWMAX = 16
RW = 256
MESH = pl.DeviceIdType.MESH
F32 = jnp.float32
BF16 = jnp.bfloat16

PARTNERS = (
    (0, 2), (2, 0), (1, 3), (3, 1), (0, 1), (2, 2), (1, 0), (3, 3),
    (0, 3), (1, 2), (3, 0), (2, 1), (1, 1), (2, 3), (3, 2),
)
SIDE = 4
MARGIN = 8
LANES = 128
AHEAD = 2
MEDGE = 384


def cubic_taps(fraction):
    t = fraction.astype(F32) / 256.0
    t2 = t * t
    t3 = t2 * t
    return (
        (-t3 + 2.0 * t2 - t) * 0.5,
        (3.0 * t3 - 5.0 * t2 + 2.0) * 0.5,
        (-3.0 * t3 + 4.0 * t2 + t) * 0.5,
        (t3 - t2) * 0.5,
    )


def ramp_tile(shift):
    rows = lax.broadcasted_iota(jnp.int32, (RW, RW), 0)
    cols = lax.broadcasted_iota(jnp.int32, (RW, RW), 1)
    n = rows - cols + shift
    odd = (n & 1) == 1
    safe = jnp.where(n == 0, 1, n).astype(F32)
    value = jnp.where(n == 0, 0.25, jnp.where(odd, -1.0 / (math.pi**2 * safe * safe), 0.0))
    return jnp.where(jnp.abs(n) <= RW, value, 0.0)


def exchange_kernel(
    proj, offset, doff_in, dfrac_in,
    sino, halo_l, halo_r, mean, ramp,
    pbuf, obuf, doff, dfrac, padded, lev, sent, got, al,
    d_sem, p_sem, o_sem, es_sem, er_sem, own_sem, s_sem, r_sem, hs_sem, hr_sem, ms_sem, mr_sem,
):
    me = lax.axis_index("ang")
    col = lax.axis_index("col")
    n_col = lax.axis_size("col")
    angles, rows, width = proj.shape
    slabs = sino.shape[0]
    slab = rows // slabs
    blocks = width // LANES
    y, x = me // SIDE, lax.rem(me, SIDE)
    sign = 1 - 2 * lax.rem(col, 2)
    left = lax.rem(col + n_col - 1, n_col)
    right = lax.rem(col + 1, n_col)

    def partner(step):
        return lax.rem(y + SIDE + sign * step[0], SIDE) * SIDE + lax.rem(x + SIDE + sign * step[1], SIDE)

    def frame_copy(a):
        return pltpu.make_async_copy(proj.at[a], pbuf.at[a], p_sem.at[a])

    drift_copies = (
        pltpu.make_async_copy(doff_in, doff, d_sem.at[0]),
        pltpu.make_async_copy(dfrac_in, dfrac, d_sem.at[1]),
    )
    for copy in drift_copies:
        copy.start()
    offset_copy = pltpu.make_async_copy(offset, obuf, o_sem)
    frame_copy(0).start()
    offset_copy.start()
    for a in range(1, angles):
        frame_copy(a).start()

    barrier = pltpu.get_barrier_semaphore()
    for step in PARTNERS:
        pl.semaphore_signal(barrier, 1, device_id={"ang": partner(step)}, device_id_type=MESH)
    for neighbour in (left, right):
        pl.semaphore_signal(barrier, 1, device_id={"col": neighbour}, device_id_type=MESH)

    zeros = jnp.zeros((blocks, MARGIN, LANES), F32)
    padded[:, 0:MARGIN, :] = zeros
    padded[:, MARGIN + rows : 2 * MARGIN + rows, :] = zeros

    def edge_copies(a):
        return (
            pltpu.make_async_remote_copy(
                sent.at[a, 1], got.at[a, 0], es_sem.at[a, 0], er_sem.at[a, 0],
                device_id={"col": right}, device_id_type=MESH,
            ),
            pltpu.make_async_remote_copy(
                sent.at[a, 0], got.at[a, 1], es_sem.at[a, 1], er_sem.at[a, 1],
                device_id={"col": left}, device_id_type=MESH,
            ),
        )

    def level(a):
        frame_copy(a).wait()
        shift = doff[0, me * angles + a]
        taps = cubic_taps(dfrac[0, me * angles + a])

        def fill(j, carry):
            at = pl.multiple_of(j * slab, slab)
            for b in range(blocks):
                lanes = pl.ds(b * LANES, LANES)
                padded[b, pl.ds(at + MARGIN, slab), :] = (
                    pbuf[a, pl.ds(at, slab), lanes].astype(F32) + obuf[pl.ds(at, slab), lanes]
                )
            return carry

        lax.fori_loop(0, slabs, fill, 0)

        def mix(j, carry):
            at = pl.multiple_of(j * slab, slab)
            base = at + (MARGIN - 1) + shift
            total = taps[0] * padded[:, pl.ds(base, slab), :]
            for k in range(1, 4):
                total = total + taps[k] * padded[:, pl.ds(base + k, slab), :]
            total = total.astype(BF16)
            sent[a, 0, pl.ds(at, slab), :] = total[0]
            sent[a, 1, pl.ds(at, slab), :] = total[blocks - 1]
            lev[lax.rem(a, AHEAD + 1), pl.ds(1, blocks), pl.ds(at, slab), :] = total.astype(F32)
            return carry

        lax.fori_loop(0, slabs, mix, 0)

    def align(a):
        shift = doff[1, me * angles + a]
        taps = cubic_taps(dfrac[1, me * angles + a])
        slot = lax.rem(a, AHEAD + 1)
        lane = lax.broadcasted_iota(jnp.int32, (1, slab, LANES), 2)

        def mix(j, carry):
            at = pl.multiple_of(j * slab, slab)
            total = None
            for k in range(4):
                moved = shift + (k - 1)
                back = jnp.where(moved < 0, 1, 0)
                turn = moved + back * LANES
                block = lev[slot, pl.ds(1 - back, blocks + 1), pl.ds(at, slab), :]
                rolled = pltpu.roll(block, lax.rem(LANES - turn, LANES), 2)
                piece = taps[k] * jnp.where(lane < LANES - turn, rolled[0:blocks], rolled[1 : blocks + 1])
                total = piece if total is None else total + piece
            out = total.astype(BF16)
            for b in range(blocks):
                al[a, j, :, pl.ds(b * LANES, LANES)] = out[b]
            return carry

        lax.fori_loop(0, slabs, mix, 0)

    def send(a):
        for step in PARTNERS:
            j = partner(step)
            pltpu.make_async_remote_copy(
                al.at[a, j], sino.at[me, a], s_sem.at[a], r_sem.at[a],
                device_id={"ang": j}, device_id_type=MESH,
            ).start()
        pltpu.make_async_copy(al.at[a, me], sino.at[me, a], own_sem.at[a]).start()

    def level_and_send(a):
        level(a)
        for copy in edge_copies(a):
            copy.start()

    def finish(a):
        for copy in edge_copies(a):
            copy.wait_recv()
        slot = lax.rem(a, AHEAD + 1)
        lev[slot, 0] = jnp.where(col > 0, got[a, 0].astype(F32), 0.0)
        lev[slot, blocks + 1] = jnp.where(col < n_col - 1, got[a, 1].astype(F32), 0.0)
        align(a)
        send(a)

    for copy in drift_copies:
        copy.wait()
    offset_copy.wait()
    level(0)
    pl.semaphore_wait(barrier, len(PARTNERS) + 2)
    for copy in edge_copies(0):
        copy.start()
    for a in range(1, AHEAD):
        level_and_send(a)

    def both(a, carry):
        finish(a)
        level_and_send(a + AHEAD)
        return carry

    lax.fori_loop(0, angles - AHEAD, both, 0)

    def last(a, carry):
        finish(a)
        return carry

    lax.fori_loop(angles - AHEAD, angles, last, 0)

    for k in range(3):
        ramp[k] = ramp_tile(RW * (k - 1)).astype(BF16)

    def halo_copies(k):
        return (
            pltpu.make_async_remote_copy(
                sino.at[:, k, :, pl.ds(width - RW, RW)], halo_l.at[:, k], hs_sem.at[0], hr_sem.at[0],
                device_id={"col": right}, device_id_type=MESH,
            ),
            pltpu.make_async_remote_copy(
                sino.at[:, k, :, pl.ds(0, RW)], halo_r.at[:, k], hs_sem.at[1], hr_sem.at[1],
                device_id={"col": left}, device_id_type=MESH,
            ),
        )

    def arrived(k):
        return pltpu.make_async_remote_copy(
            al.at[k, pl.ds(0, slabs - 1)], sino.at[pl.ds(0, slabs - 1), k], s_sem.at[k], r_sem.at[k],
            device_id={"ang": me}, device_id_type=MESH,
        )

    def collect(k, total):
        pltpu.make_async_copy(al.at[k, me], sino.at[me, k], own_sem.at[k]).wait()
        arrived(k).wait_recv()
        for copy in halo_copies(k):
            copy.start()
        return lax.fori_loop(0, slabs, lambda i, t: t + sino[i, k].astype(F32), total)

    total = lax.fori_loop(0, angles, collect, jnp.zeros((slab, width), F32))
    mean[:, pl.ds(MEDGE, width)] = total / float(slabs * angles)

    mean_copies = (
        pltpu.make_async_remote_copy(
            mean.at[:, pl.ds(width, MEDGE)], mean.at[:, pl.ds(0, MEDGE)], ms_sem.at[0], mr_sem.at[0],
            device_id={"col": right}, device_id_type=MESH,
        ),
        pltpu.make_async_remote_copy(
            mean.at[:, pl.ds(MEDGE, MEDGE)], mean.at[:, pl.ds(MEDGE + width, MEDGE)], ms_sem.at[1], mr_sem.at[1],
            device_id={"col": left}, device_id_type=MESH,
        ),
    )
    for copy in mean_copies:
        copy.start()

    def drain(k, carry):
        arrived(k).wait_send()
        for copy in edge_copies(k):
            copy.wait_send()
        return carry

    lax.fori_loop(0, angles, drain, 0)
    for side, halo in ((0, halo_l), (1, halo_r)):
        whole = pltpu.make_async_remote_copy(
            halo, halo, hs_sem.at[side], hr_sem.at[side], device_id={"col": left}, device_id_type=MESH
        )
        whole.wait_send()
        whole.wait_recv()
    for copy in mean_copies:
        copy.wait_send()
        copy.wait_recv()


def filter_kernel(
    sino, halo_l, halo_r, mean, ramp, widths,
    out,
    ends, cyc, kept, obuf, o_sem,
):
    col = lax.axis_index("col")
    n_col = lax.axis_size("col")
    slabs, angles, slab, width = sino.shape
    total_cols = n_col * width
    parts = width // RW

    ends[0] = jnp.where(col > 0, ramp[0], jnp.zeros((RW, RW), BF16))
    ends[1] = jnp.where(col < n_col - 1, ramp[2], jnp.zeros((RW, RW), BF16))

    span = width + 2 * MEDGE
    at = lax.broadcasted_iota(jnp.int32, (slab, span), 1) + (col * width - MEDGE)
    inside = (at >= 0) & (at < total_cols)
    line = lax.broadcasted_iota(jnp.int32, (slab, 1), 0)
    half = jnp.zeros((slab, 1), jnp.int32)
    for r in range(slab):
        half = jnp.where(line == r, widths[r], half)
    centre = jnp.where(inside, mean[...], 0.0)
    running = centre
    for j in range(1, BWMAX + 1):
        pair = pltpu.roll(centre, j, 1) + pltpu.roll(centre, span - j, 1)
        running = running + jnp.where(half >= j, pair, 0.0)
    count = jnp.minimum(at, half) + jnp.minimum(total_cols - 1 - at, half) + 1
    count = jnp.maximum(count, 1).astype(F32)
    cycle = jnp.where(inside, centre - running / count, 0.0)
    first = cycle.astype(BF16)
    rest = cycle - first.astype(F32)
    second = rest.astype(BF16)
    third = (rest - second.astype(F32)).astype(BF16)
    cyc[0:slab] = first
    cyc[slab : 2 * slab] = second
    cyc[2 * slab : 3 * slab] = third
    for n in range(parts):
        acc = jnp.zeros((3 * slab, RW), F32)
        for k in range(3):
            acc = acc + jnp.dot(
                cyc[:, pl.ds(MEDGE + RW * (n + k - 1), RW)], ramp[k], preferred_element_type=F32
            )
        kept[:, pl.ds(n * RW, RW)] = acc[0:slab] + acc[slab : 2 * slab] + acc[2 * slab : 3 * slab]

    group = obuf.shape[1]
    steps = slabs // group

    def put(g):
        slot = lax.rem(g, 2)
        return pltpu.make_async_copy(obuf.at[slot], out.at[pl.ds(g * group, group)], o_sem.at[slot])

    lines = group * angles * slab

    def filt(g, carry):
        slot = lax.rem(g, 2)

        @pl.when(g >= 2)
        def _():
            put(g - 2).wait()

        def window(m):
            if m < 0:
                return halo_l[pl.ds(g * group, group)].reshape(lines, RW)
            if m == parts:
                return halo_r[pl.ds(g * group, group)].reshape(lines, RW)
            return sino[pl.ds(g * group, group), :, :, pl.ds(m * RW, RW)].reshape(lines, RW)

        for n in range(parts):
            acc = jnp.dot(window(n), ramp[1], preferred_element_type=F32)
            acc = acc + jnp.dot(window(n - 1), ends[0] if n == 0 else ramp[0], preferred_element_type=F32)
            acc = acc + jnp.dot(
                window(n + 1), ends[1] if n == parts - 1 else ramp[2], preferred_element_type=F32
            )
            lanes = pl.ds(n * RW, RW)
            obuf[slot, :, :, :, lanes] = acc.reshape(group, angles, slab, RW) - kept[:, lanes]
        put(g).start()
        return carry

    lax.fori_loop(0, steps, filt, 0)
    put(steps - 2).wait()
    put(steps - 1).wait()


def on_device(projections, detector_offset, drift_offsets, drift_fractions, cycle_widths):
    angles, rows, width = projections.shape
    slab = cycle_widths.shape[0]
    slabs = rows // slab
    blocks = width // LANES
    vmem = pl.BlockSpec(memory_space=pltpu.VMEM)
    smem = pl.BlockSpec(memory_space=pltpu.SMEM)
    hbm = pl.BlockSpec(memory_space=pltpu.HBM)
    dma = pltpu.SemaphoreType.DMA
    held = pl.pallas_call(
        exchange_kernel,
        name="exchange",
        out_shape=(
            pltpu.VMEM((slabs, angles, slab, width), BF16),
            pltpu.VMEM((slabs, angles, slab, RW), BF16),
            pltpu.VMEM((slabs, angles, slab, RW), BF16),
            pltpu.VMEM((slab, width + 2 * MEDGE), F32),
            pltpu.VMEM((3, RW, RW), BF16),
        ),
        in_specs=[hbm] * 4,
        out_specs=(vmem,) * 5,
        scratch_shapes=[
            pltpu.VMEM((angles, rows, width), BF16),
            pltpu.VMEM((rows, width), F32),
            pltpu.SMEM(drift_offsets.shape, jnp.int32),
            pltpu.SMEM(drift_offsets.shape, jnp.int32),
            pltpu.VMEM((blocks, rows + 2 * MARGIN, LANES), F32),
            pltpu.VMEM((AHEAD + 1, blocks + 2, rows, LANES), F32),
            pltpu.VMEM((angles, 2, rows, LANES), BF16),
            pltpu.VMEM((angles, 2, rows, LANES), BF16),
            pltpu.VMEM((angles, slabs, slab, width), BF16),
            dma((2,)),
            dma((angles,)),
            dma,
            dma((angles, 2)),
            dma((angles, 2)),
            dma((angles,)),
            dma((angles,)),
            dma((angles,)),
            dma((2,)),
            dma((2,)),
            dma((2,)),
            dma((2,)),
        ],
        compiler_params=pltpu.CompilerParams(
            collective_id=0, has_side_effects=True, vmem_limit_bytes=44 * 1024 * 1024
        ),
        cost_estimate=pl.CostEstimate(flops=40_000_000, bytes_accessed=6 * 1024 * 1024, transcendentals=0),
    )(projections, detector_offset, drift_offsets, drift_fractions)
    group = 2
    filtered = pl.pallas_call(
        filter_kernel,
        name="filter",
        out_shape=jax.ShapeDtypeStruct((slabs, angles, slab, width), F32),
        in_specs=[vmem] * 5 + [smem],
        out_specs=hbm,
        scratch_shapes=[
            pltpu.VMEM((2, RW, RW), BF16),
            pltpu.VMEM((3 * slab, width + 2 * MEDGE), BF16),
            pltpu.VMEM((slab, width), F32),
            pltpu.VMEM((2, group, angles, slab, width), F32),
            dma((2,)),
        ],
        compiler_params=pltpu.CompilerParams(vmem_limit_bytes=24 * 1024 * 1024),
        cost_estimate=pl.CostEstimate(flops=3_300_000_000, bytes_accessed=8 * 1024 * 1024, transcendentals=0),
    )(*held, cycle_widths)
    return filtered.reshape(slabs * angles, slab, width)


def solution(mesh):
    placed = (P("ang", None, "col"), P(None, "col"), P(), P(), P("ang"))
    return jax.shard_map(
        on_device, mesh=mesh, in_specs=placed, out_specs=P(None, "ang", "col"), check_vma=False
    )
```

profile of v0, /device:TPU:0, one launch (start us, length us, event | category | flops | bytes accessed | tf_op | source)
XLA Modules:
  0.0 76.7 jit_solution(11386357637887562282)
XLA Ops:
  0.0 0.0 copy-start
  0.0 1.2 %copy-done = f32[256,1024]{1,0:T(8,128)S(1)} copy-done((f32[256,1024]{1,0:T(8,128)S(1)}, f32[256,1024]{1,0:T(8,128)}, u32[]{:S(2)}) %copy-start) | copy-done | bytes 1048600
  1.2 0.0 copy-start.1
  1.2 0.7 copy-done.1
  1.9 0.0 copy-start.2
  1.9 0.7 copy-done.2
  2.6 0.0 copy-start.3
  2.6 65.4 %exchange.1 = (bf16[16,8,16,1024]{3,2,1,0:T(8,128)(2,1)S(1)}, bf16[16,8,16,256]{3,2,1,0:T(8,128)(2,1)S(1)}, bf16[16,8,16,256]{3,2,1,0:T(8,128)(2,1)S(1)}, f32[16,1792]{1,0:T(8,128)S(1)}, bf16[3,256,256]{2,1,0:T(8,128)(2,1)S(1)}) custom-call(bf16[8,256,1024]{2,1,0:T(8,128)(2,1)} %proj.1, f32[256,1024]{1,0:T(8,128)S(1)} %copy-done, s32[2,128]{1,0:T(2,128)S(1)} %copy-done.1, ...), custom_call_target="tpu_custom_call" | custom-call | flops 40000000 | bytes 6291456 | tf_op jit(solution)/shard_map/exchange/pallas_call | solution.py:362
  68.0 0.0 copy-done.3
  68.0 8.7 %filter.1 = f32[16,8,16,1024]{3,2,1,0:T(8,128)} custom-call(bf16[16,8,16,1024]{3,2,1,0:T(8,128)(2,1)S(1)} %get-tuple-element.10.sino, bf16[16,8,16,256]{3,2,1,0:T(8,128)(2,1)S(1)} %get-tuple-element.11.halo_l, bf16[16,8,16,256]{3,2,1,0:T(8,128)(2,1)S(1)} %get-tuple-element.12.halo_r, f32[16,1792]{1,0:T(8,128)S(1)} %get-tuple-element.13.mean, ...), custom_call_target="tpu_custom_call" | custom-call | flops 3300000000 | bytes 8388608 | tf_op jit(solution)/shard_map/filter/pallas_call | solution.py:403
Async XLA Ops:
  0.0 1.2 %copy-start = (f32[256,1024]{1,0:T(8,128)S(1)}, f32[256,1024]{1,0:T(8,128)}, u32[]{:S(2)}) copy-start(f32[256,1024]{1,0:T(8,128)} %offset.1) | copy-start | bytes 3145732
  1.2 0.7 copy-start.1
  1.9 0.7 copy-start.2
  2.6 65.4 %copy-start.3 = (s32[16]{0:T(128)S(1)}, s32[16]{0:T(128)}, u32[]{:S(2)}) copy-start(s32[16]{0:T(128)} %widths.1) | copy-start | bytes 196
where the time goes:
time: 76.9 us; the launch traced here: 76.7 us
  Pallas kernels  74.1 us (96%)
  local copies, waits for them, and re-layouts  2.58 us (3%)
    pallas_call x1, Pallas kernels, on_device(): pl.pallas_call(exchange_kernel, name='exchange', out_shape=(pltpu.VMEM((s...  65.4 us
    pallas_call x1, Pallas kernels, on_device(): pl.pallas_call(filter_kernel, name='filter', out_shape=jax.ShapeDtypeStru...  8.69 us
    unnamed x8, local copies, waits for them, and re-layouts  2.58 us

commit v1 on v0

--- a/solution.py
+++ b/solution.py
@@ -14,10 +14,7 @@
 F32 = jnp.float32
 BF16 = jnp.bfloat16
 
-PARTNERS = (
-    (0, 2), (2, 0), (1, 3), (3, 1), (0, 1), (2, 2), (1, 0), (3, 3),
-    (0, 3), (1, 2), (3, 0), (2, 1), (1, 1), (2, 3), (3, 2),
-)
+STRIDE = 7
 SIDE = 4
 MARGIN = 8
 LANES = 128
@@ -48,25 +45,27 @@
 
 
 def exchange_kernel(
-    proj, offset, doff_in, dfrac_in,
-    sino, halo_l, halo_r, mean, ramp,
-    pbuf, obuf, doff, dfrac, padded, lev, sent, got, al,
+    proj, offset, doff_in, dfrac_in, widths_in,
+    part, kept,
+    pbuf, obuf, doff, dfrac, widths, padded, lev, sent, got, al, sino, halo_l, halo_r, mean, cyc, ramp, ends,
     d_sem, p_sem, o_sem, es_sem, er_sem, own_sem, s_sem, r_sem, hs_sem, hr_sem, ms_sem, mr_sem,
 ):
     me = lax.axis_index("ang")
     col = lax.axis_index("col")
     n_col = lax.axis_size("col")
     angles, rows, width = proj.shape
-    slabs = sino.shape[0]
-    slab = rows // slabs
+    slabs, _, slab, _ = sino.shape
     blocks = width // LANES
     y, x = me // SIDE, lax.rem(me, SIDE)
     sign = 1 - 2 * lax.rem(col, 2)
     left = lax.rem(col + n_col - 1, n_col)
     right = lax.rem(col + 1, n_col)
 
-    def partner(step):
-        return lax.rem(y + SIDE + sign * step[0], SIDE) * SIDE + lax.rem(x + SIDE + sign * step[1], SIDE)
+    def partner(n):
+        place = lax.rem(STRIDE * n, slabs)
+        return lax.rem(y + SIDE + sign * (place // SIDE), SIDE) * SIDE + lax.rem(
+            x + SIDE + sign * lax.rem(place, SIDE), SIDE
+        )
 
     def frame_copy(a):
         return pltpu.make_async_copy(proj.at[a], pbuf.at[a], p_sem.at[a])
@@ -74,6 +73,7 @@
     drift_copies = (
         pltpu.make_async_copy(doff_in, doff, d_sem.at[0]),
         pltpu.make_async_copy(dfrac_in, dfrac, d_sem.at[1]),
+        pltpu.make_async_copy(widths_in, widths, d_sem.at[2]),
     )
     for copy in drift_copies:
         copy.start()
@@ -84,8 +84,8 @@
         frame_copy(a).start()
 
     barrier = pltpu.get_barrier_semaphore()
-    for step in PARTNERS:
-        pl.semaphore_signal(barrier, 1, device_id={"ang": partner(step)}, device_id_type=MESH)
+    for n in range(1, slabs):
+        pl.semaphore_signal(barrier, 1, device_id={"ang": partner(n)}, device_id_type=MESH)
     for neighbour in (left, right):
         pl.semaphore_signal(barrier, 1, device_id={"col": neighbour}, device_id_type=MESH)
 
@@ -135,13 +135,14 @@
 
         lax.fori_loop(0, slabs, mix, 0)
 
-    def align(a):
+    def align_and_send(a):
         shift = doff[1, me * angles + a]
         taps = cubic_taps(dfrac[1, me * angles + a])
         slot = lax.rem(a, AHEAD + 1)
         lane = lax.broadcasted_iota(jnp.int32, (1, slab, LANES), 2)
 
-        def mix(j, carry):
+        def mix(n, carry):
+            j = partner(n)
             at = pl.multiple_of(j * slab, slab)
             total = None
             for k in range(4):
@@ -155,17 +156,18 @@
             out = total.astype(BF16)
             for b in range(blocks):
                 al[a, j, :, pl.ds(b * LANES, LANES)] = out[b]
+
+            @pl.when(n > 1)
+            def _():
+                to = partner(n - 1)
+                pltpu.make_async_remote_copy(
+                    al.at[a, to], sino.at[me, a], s_sem.at[a], r_sem.at[a],
+                    device_id={"ang": to}, device_id_type=MESH,
+                ).start()
+
             return carry
 
-        lax.fori_loop(0, slabs, mix, 0)
-
-    def send(a):
-        for step in PARTNERS:
-            j = partner(step)
-            pltpu.make_async_remote_copy(
-                al.at[a, j], sino.at[me, a], s_sem.at[a], r_sem.at[a],
-                device_id={"ang": j}, device_id_type=MESH,
-            ).start()
+        lax.fori_loop(1, slabs + 1, mix, 0)
         pltpu.make_async_copy(al.at[a, me], sino.at[me, a], own_sem.at[a]).start()
 
     def level_and_send(a):
@@ -179,14 +181,13 @@
         slot = lax.rem(a, AHEAD + 1)
         lev[slot, 0] = jnp.where(col > 0, got[a, 0].astype(F32), 0.0)
         lev[slot, blocks + 1] = jnp.where(col < n_col - 1, got[a, 1].astype(F32), 0.0)
-        align(a)
-        send(a)
+        align_and_send(a)
 
     for copy in drift_copies:
         copy.wait()
     offset_copy.wait()
     level(0)
-    pl.semaphore_wait(barrier, len(PARTNERS) + 2)
+    pl.semaphore_wait(barrier, slabs + 1)
     for copy in edge_copies(0):
         copy.start()
     for a in range(1, AHEAD):
@@ -208,14 +209,17 @@
     for k in range(3):
         ramp[k] = ramp_tile(RW * (k - 1)).astype(BF16)
 
+    ends[0] = jnp.where(col > 0, ramp[0], jnp.zeros((RW, RW), BF16))
+    ends[1] = jnp.where(col < n_col - 1, ramp[2], jnp.zeros((RW, RW), BF16))
+
     def halo_copies(k):
         return (
             pltpu.make_async_remote_copy(
-                sino.at[:, k, :, pl.ds(width - RW, RW)], halo_l.at[:, k], hs_sem.at[0], hr_sem.at[0],
+                sino.at[:, k, :, pl.ds(width - RW, RW)], halo_l.at[:, k], hs_sem.at[0], hr_sem.at[0, k],
                 device_id={"col": right}, device_id_type=MESH,
             ),
             pltpu.make_async_remote_copy(
-                sino.at[:, k, :, pl.ds(0, RW)], halo_r.at[:, k], hs_sem.at[1], hr_sem.at[1],
+                sino.at[:, k, :, pl.ds(0, RW)], halo_r.at[:, k], hs_sem.at[1], hr_sem.at[1, k],
                 device_id={"col": left}, device_id_type=MESH,
             ),
         )
@@ -229,11 +233,44 @@
     def collect(k, total):
         pltpu.make_async_copy(al.at[k, me], sino.at[me, k], own_sem.at[k]).wait()
         arrived(k).wait_recv()
+        return lax.fori_loop(0, slabs, lambda i, t: t + sino[i, k].astype(F32), total)
+
+    def pass_on(k):
         for copy in halo_copies(k):
             copy.start()
-        return lax.fori_loop(0, slabs, lambda i, t: t + sino[i, k].astype(F32), total)
-
-    total = lax.fori_loop(0, angles, collect, jnp.zeros((slab, width), F32))
+
+    parts = width // RW
+
+    def filt(k):
+        for copy in halo_copies(k):
+            copy.wait_recv()
+
+        def window(m):
+            if m < 0:
+                return halo_l[:, k].reshape(rows, RW)
+            if m == parts:
+                return halo_r[:, k].reshape(rows, RW)
+            return sino[:, k, :, pl.ds(m * RW, RW)].reshape(rows, RW)
+
+        for n in range(parts):
+            acc = jnp.dot(window(n), ramp[1], preferred_element_type=F32)
+            acc = acc + jnp.dot(window(n - 1), ends[0] if n == 0 else ramp[0], preferred_element_type=F32)
+            acc = acc + jnp.dot(
+                window(n + 1), ends[1] if n == parts - 1 else ramp[2], preferred_element_type=F32
+            )
+            part[:, k, :, pl.ds(n * RW, RW)] = acc.reshape(slabs, slab, RW)
+
+    total = collect(0, jnp.zeros((slab, width), F32))
+    pass_on(0)
+
+    def middle(k, total):
+        total = collect(k, total)
+        pass_on(k)
+        filt(k - 1)
+        return total
+
+    total = lax.fori_loop(1, angles - 1, middle, total)
+    total = collect(angles - 1, total)
     mean[:, pl.ds(MEDGE, width)] = total / float(slabs * angles)
 
     mean_copies = (
@@ -248,6 +285,8 @@
     )
     for copy in mean_copies:
         copy.start()
+    pass_on(angles - 1)
+    filt(angles - 2)
 
     def drain(k, carry):
         arrived(k).wait_send()
@@ -256,31 +295,10 @@
         return carry
 
     lax.fori_loop(0, angles, drain, 0)
-    for side, halo in ((0, halo_l), (1, halo_r)):
-        whole = pltpu.make_async_remote_copy(
-            halo, halo, hs_sem.at[side], hr_sem.at[side], device_id={"col": left}, device_id_type=MESH
-        )
-        whole.wait_send()
-        whole.wait_recv()
     for copy in mean_copies:
-        copy.wait_send()
         copy.wait_recv()
 
-
-def filter_kernel(
-    sino, halo_l, halo_r, mean, ramp, widths,
-    out,
-    ends, cyc, kept, obuf, o_sem,
-):
-    col = lax.axis_index("col")
-    n_col = lax.axis_size("col")
-    slabs, angles, slab, width = sino.shape
     total_cols = n_col * width
-    parts = width // RW
-
-    ends[0] = jnp.where(col > 0, ramp[0], jnp.zeros((RW, RW), BF16))
-    ends[1] = jnp.where(col < n_col - 1, ramp[2], jnp.zeros((RW, RW), BF16))
-
     span = width + 2 * MEDGE
     at = lax.broadcasted_iota(jnp.int32, (slab, span), 1) + (col * width - MEDGE)
     inside = (at >= 0) & (at < total_cols)
@@ -311,43 +329,32 @@
             )
         kept[:, pl.ds(n * RW, RW)] = acc[0:slab] + acc[slab : 2 * slab] + acc[2 * slab : 3 * slab]
 
-    group = obuf.shape[1]
-    steps = slabs // group
-
-    def put(g):
-        slot = lax.rem(g, 2)
-        return pltpu.make_async_copy(obuf.at[slot], out.at[pl.ds(g * group, group)], o_sem.at[slot])
-
-    lines = group * angles * slab
-
-    def filt(g, carry):
-        slot = lax.rem(g, 2)
-
-        @pl.when(g >= 2)
-        def _():
-            put(g - 2).wait()
-
-        def window(m):
-            if m < 0:
-                return halo_l[pl.ds(g * group, group)].reshape(lines, RW)
-            if m == parts:
-                return halo_r[pl.ds(g * group, group)].reshape(lines, RW)
-            return sino[pl.ds(g * group, group), :, :, pl.ds(m * RW, RW)].reshape(lines, RW)
-
-        for n in range(parts):
-            acc = jnp.dot(window(n), ramp[1], preferred_element_type=F32)
-            acc = acc + jnp.dot(window(n - 1), ends[0] if n == 0 else ramp[0], preferred_element_type=F32)
-            acc = acc + jnp.dot(
-                window(n + 1), ends[1] if n == parts - 1 else ramp[2], preferred_element_type=F32
-            )
-            lanes = pl.ds(n * RW, RW)
-            obuf[slot, :, :, :, lanes] = acc.reshape(group, angles, slab, RW) - kept[:, lanes]
-        put(g).start()
+    filt(angles - 1)
+    for side, halo in ((0, halo_l), (1, halo_r)):
+        pltpu.make_async_remote_copy(
+            halo, halo, hs_sem.at[side], hr_sem.at[side, 0], device_id={"col": left}, device_id_type=MESH
+        ).wait_send()
+    for copy in mean_copies:
+        copy.wait_send()
+
+
+def subtract_kernel(part, kept, out, obuf, o_sem):
+    slabs = part.shape[0]
+
+    def put(i):
+        return pltpu.make_async_copy(obuf.at[i], out.at[i], o_sem.at[i])
+
+    def step(i, carry):
+        obuf[i] = part[i] - kept[...]
+        put(i).start()
         return carry
 
-    lax.fori_loop(0, steps, filt, 0)
-    put(steps - 2).wait()
-    put(steps - 1).wait()
+    def wait(i, carry):
+        put(i).wait()
+        return carry
+
+    lax.fori_loop(0, slabs, step, 0)
+    lax.fori_loop(0, slabs, wait, 0)
 
 
 def on_device(projections, detector_offset, drift_offsets, drift_fractions, cycle_widths):
@@ -356,32 +363,37 @@
     slabs = rows // slab
     blocks = width // LANES
     vmem = pl.BlockSpec(memory_space=pltpu.VMEM)
-    smem = pl.BlockSpec(memory_space=pltpu.SMEM)
     hbm = pl.BlockSpec(memory_space=pltpu.HBM)
     dma = pltpu.SemaphoreType.DMA
-    held = pl.pallas_call(
+    given = (projections, detector_offset, drift_offsets, drift_fractions, cycle_widths)
+    part, kept = pl.pallas_call(
         exchange_kernel,
         name="exchange",
         out_shape=(
-            pltpu.VMEM((slabs, angles, slab, width), BF16),
-            pltpu.VMEM((slabs, angles, slab, RW), BF16),
-            pltpu.VMEM((slabs, angles, slab, RW), BF16),
-            pltpu.VMEM((slab, width + 2 * MEDGE), F32),
-            pltpu.VMEM((3, RW, RW), BF16),
+            pltpu.VMEM((slabs, angles, slab, width), F32),
+            pltpu.VMEM((slab, width), F32),
         ),
-        in_specs=[hbm] * 4,
-        out_specs=(vmem,) * 5,
+        in_specs=[hbm] * 5,
+        out_specs=(vmem,) * 2,
         scratch_shapes=[
             pltpu.VMEM((angles, rows, width), BF16),
             pltpu.VMEM((rows, width), F32),
             pltpu.SMEM(drift_offsets.shape, jnp.int32),
             pltpu.SMEM(drift_offsets.shape, jnp.int32),
+            pltpu.SMEM(cycle_widths.shape, jnp.int32),
             pltpu.VMEM((blocks, rows + 2 * MARGIN, LANES), F32),
             pltpu.VMEM((AHEAD + 1, blocks + 2, rows, LANES), F32),
             pltpu.VMEM((angles, 2, rows, LANES), BF16),
             pltpu.VMEM((angles, 2, rows, LANES), BF16),
             pltpu.VMEM((angles, slabs, slab, width), BF16),
-            dma((2,)),
+            pltpu.VMEM((slabs, angles, slab, width), BF16),
+            pltpu.VMEM((slabs, angles, slab, RW), BF16),
+            pltpu.VMEM((slabs, angles, slab, RW), BF16),
+            pltpu.VMEM((slab, width + 2 * MEDGE), F32),
+            pltpu.VMEM((3 * slab, width + 2 * MEDGE), BF16),
+            pltpu.VMEM((3, RW, RW), BF16),
+            pltpu.VMEM((2, RW, RW), BF16),
+            dma((3,)),
             dma((angles,)),
             dma,
             dma((angles, 2)),
@@ -390,32 +402,23 @@
             dma((angles,)),
             dma((angles,)),
             dma((2,)),
-            dma((2,)),
+            dma((2, angles)),
             dma((2,)),
             dma((2,)),
         ],
         compiler_params=pltpu.CompilerParams(
-            collective_id=0, has_side_effects=True, vmem_limit_bytes=44 * 1024 * 1024
+            collective_id=0, has_side_effects=True, vmem_limit_bytes=54 * 1024 * 1024
         ),
-        cost_estimate=pl.CostEstimate(flops=40_000_000, bytes_accessed=6 * 1024 * 1024, transcendentals=0),
-    )(projections, detector_offset, drift_offsets, drift_fractions)
-    group = 2
+    )(*(pltpu.with_memory_space_constraint(a, pltpu.HBM) for a in given))
     filtered = pl.pallas_call(
-        filter_kernel,
-        name="filter",
+        subtract_kernel,
+        name="subtract",
         out_shape=jax.ShapeDtypeStruct((slabs, angles, slab, width), F32),
-        in_specs=[vmem] * 5 + [smem],
+        in_specs=[vmem] * 2,
         out_specs=hbm,
-        scratch_shapes=[
-            pltpu.VMEM((2, RW, RW), BF16),
-            pltpu.VMEM((3 * slab, width + 2 * MEDGE), BF16),
-            pltpu.VMEM((slab, width), F32),
-            pltpu.VMEM((2, group, angles, slab, width), F32),
-            dma((2,)),
-        ],
+        scratch_shapes=[pltpu.VMEM((slabs, angles, slab, width), F32), dma((slabs,))],
         compiler_params=pltpu.CompilerParams(vmem_limit_bytes=24 * 1024 * 1024),
-        cost_estimate=pl.CostEstimate(flops=3_300_000_000, bytes_accessed=8 * 1024 * 1024, transcendentals=0),
-    )(*held, cycle_widths)
+    )(part, kept)
     return filtered.reshape(slabs * angles, slab, width)
 
 

time: 76.9 us -> 67.5 us (0.88)
  Pallas kernels: 74.1 us -> 67.4 us
  local copies, waits for them, and re-layouts: 2.58 us -> 0 us
    pallas_call x1, Pallas kernels: 8.69 us -> 3.45 us  [on_device(): pl.pallas_call(subtract_kernel, name='subtract', out_shape=jax.ShapeDtype...]
    unnamed x8 -> x0, local copies, waits for them, and re-layouts: 2.58 us -> none
    pallas_call x1, Pallas kernels: 65.4 us -> 63.9 us  [on_device(): pl.pallas_call(exchange_kernel, name='exchange', out_shape=(pltpu.VMEM((s...]
where the time goes in v1:
time: 67.5 us; the launch traced here: 67.4 us
  Pallas kernels  67.4 us (100%)
    pallas_call x1, Pallas kernels, on_device(): pl.pallas_call(exchange_kernel, name='exchange', out_shape=(pltpu.VMEM((s...  63.9 us
    pallas_call x1, Pallas kernels, on_device(): pl.pallas_call(subtract_kernel, name='subtract', out_shape=jax.ShapeDtype...  3.45 us

profile of v1, /device:TPU:0, one launch (start us, length us, event | category | flops | bytes accessed | tf_op | source)
XLA Modules:
  0.0 67.4 jit_solution(766076158087243847)
XLA Ops:
  0.0 63.9 %exchange.1 = (f32[16,8,16,1024]{3,2,1,0:T(8,128)S(1)}, f32[16,1024]{1,0:T(8,128)S(1)}) custom-call(bf16[8,256,1024]{2,1,0:T(8,128)(2,1)} %proj.1, f32[256,1024]{1,0:T(8,128)} %offset.1, s32[2,128]{1,0:T(2,128)} %doff_in.1, s32[2,128]{1,0:T(2,128)} %dfrac_in.1, s32[16]{0:T(128)} %widths_in.1), custom_call_target="tpu_custom_call" | custom-call | tf_op jit(solution)/shard_map/exchange/pallas_call | solution.py:369
  63.9 3.5 %subtract.1 = f32[16,8,16,1024]{3,2,1,0:T(8,128)} custom-call(f32[16,8,16,1024]{3,2,1,0:T(8,128)S(1)} %get-tuple-element.7.part, f32[16,1024]{1,0:T(8,128)S(1)} %get-tuple-element.8.kept), custom_call_target="tpu_custom_call" | custom-call | tf_op jit(solution)/shard_map/subtract/pallas_call | solution.py:413

commit v2 on v1

--- a/solution.py
+++ b/solution.py
@@ -14,7 +14,8 @@
 F32 = jnp.float32
 BF16 = jnp.bfloat16
 
-STRIDE = 7
+ORDER = (10, 6, 11, 14, 9, 2, 8, 5, 15, 7, 13, 1, 4, 3, 12, 0)
+DIGITS = 7
 SIDE = 4
 MARGIN = 8
 LANES = 128
@@ -47,7 +48,7 @@
 def exchange_kernel(
     proj, offset, doff_in, dfrac_in, widths_in,
     part, kept,
-    pbuf, obuf, doff, dfrac, widths, padded, lev, sent, got, al, sino, halo_l, halo_r, mean, cyc, ramp, ends,
+    pbuf, obuf, doff, dfrac, widths, padded, lev, sent, got, al, al_outer, sino, halo_l, halo_r, mean, cyc, ramp, ends,
     d_sem, p_sem, o_sem, es_sem, er_sem, own_sem, s_sem, r_sem, hs_sem, hr_sem, ms_sem, mr_sem,
 ):
     me = lax.axis_index("ang")
@@ -62,7 +63,15 @@
     right = lax.rem(col + 1, n_col)
 
     def partner(n):
-        place = lax.rem(STRIDE * n, slabs)
+        if isinstance(n, int):
+            place = ORDER[n]
+        else:
+            place = 0
+            for first in range(0, slabs, DIGITS):
+                code = sum(p << (4 * d) for d, p in enumerate(ORDER[first : first + DIGITS]))
+                here = jnp.clip(n - first, 0, DIGITS - 1)
+                digit = lax.shift_right_logical(jnp.int32(code), 4 * here) & 15
+                place = jnp.where(n >= first, digit, place)
         return lax.rem(y + SIDE + sign * (place // SIDE), SIDE) * SIDE + lax.rem(
             x + SIDE + sign * lax.rem(place, SIDE), SIDE
         )
@@ -84,7 +93,7 @@
         frame_copy(a).start()
 
     barrier = pltpu.get_barrier_semaphore()
-    for n in range(1, slabs):
+    for n in range(slabs - 1):
         pl.semaphore_signal(barrier, 1, device_id={"ang": partner(n)}, device_id_type=MESH)
     for neighbour in (left, right):
         pl.semaphore_signal(barrier, 1, device_id={"col": neighbour}, device_id_type=MESH)
@@ -135,7 +144,14 @@
 
         lax.fori_loop(0, slabs, mix, 0)
 
-    def align_and_send(a):
+    def rows_to(to, a, buf, piece, sem):
+        lanes = pl.ds(piece[0] * LANES, piece[1] * LANES)
+        return pltpu.make_async_remote_copy(
+            buf.at[to, :, lanes], sino.at[me, a, :, lanes], s_sem.at[sem], r_sem.at[sem],
+            device_id={"ang": to}, device_id_type=MESH,
+        )
+
+    def align_and_send(a, buf, sem, made, gone):
         shift = doff[1, me * angles + a]
         taps = cubic_taps(dfrac[1, me * angles + a])
         slot = lax.rem(a, AHEAD + 1)
@@ -144,44 +160,53 @@
         def mix(n, carry):
             j = partner(n)
             at = pl.multiple_of(j * slab, slab)
-            total = None
-            for k in range(4):
-                moved = shift + (k - 1)
-                back = jnp.where(moved < 0, 1, 0)
-                turn = moved + back * LANES
-                block = lev[slot, pl.ds(1 - back, blocks + 1), pl.ds(at, slab), :]
-                rolled = pltpu.roll(block, lax.rem(LANES - turn, LANES), 2)
-                piece = taps[k] * jnp.where(lane < LANES - turn, rolled[0:blocks], rolled[1 : blocks + 1])
-                total = piece if total is None else total + piece
-            out = total.astype(BF16)
-            for b in range(blocks):
-                al[a, j, :, pl.ds(b * LANES, LANES)] = out[b]
-
-            @pl.when(n > 1)
+            for first, number in made:
+                total = None
+                for k in range(4):
+                    moved = shift + (k - 1)
+                    back = jnp.where(moved < 0, 1, 0)
+                    turn = moved + back * LANES
+                    block = lev[slot, pl.ds(first + 1 - back, number + 1), pl.ds(at, slab), :]
+                    rolled = pltpu.roll(block, lax.rem(LANES - turn, LANES), 2)
+                    piece = taps[k] * jnp.where(lane < LANES - turn, rolled[0:number], rolled[1 : number + 1])
+                    total = piece if total is None else total + piece
+                out = total.astype(BF16)
+                for b in range(number):
+                    buf[j, :, pl.ds((first + b) * LANES, LANES)] = out[b]
+
+            @pl.when(n > 0)
             def _():
-                to = partner(n - 1)
-                pltpu.make_async_remote_copy(
-                    al.at[a, to], sino.at[me, a], s_sem.at[a], r_sem.at[a],
-                    device_id={"ang": to}, device_id_type=MESH,
-                ).start()
+                for piece in gone:
+                    rows_to(partner(n - 1), a, buf, piece, sem).start()
 
             return carry
 
-        lax.fori_loop(1, slabs + 1, mix, 0)
-        pltpu.make_async_copy(al.at[a, me], sino.at[me, a], own_sem.at[a]).start()
+        lax.fori_loop(0, slabs, mix, 0)
+
+    def own_copy(a, buf, piece, sem):
+        lanes = pl.ds(piece[0] * LANES, piece[1] * LANES)
+        return pltpu.make_async_copy(buf.at[me, :, lanes], sino.at[me, a, :, lanes], own_sem.at[sem])
 
     def level_and_send(a):
         level(a)
         for copy in edge_copies(a):
             copy.start()
 
-    def finish(a):
+    def take_edges(a):
         for copy in edge_copies(a):
             copy.wait_recv()
         slot = lax.rem(a, AHEAD + 1)
         lev[slot, 0] = jnp.where(col > 0, got[a, 0].astype(F32), 0.0)
         lev[slot, blocks + 1] = jnp.where(col < n_col - 1, got[a, 1].astype(F32), 0.0)
-        align_and_send(a)
+
+    whole = (0, blocks)
+    inner = (1, blocks - 2)
+    outer = ((0, 1), (blocks - 1, 1))
+    rim = MEDGE // LANES
+    rims = ((0, rim), (blocks - rim, rim))
+    core = (rim, blocks - 2 * rim)
+    late = angles - 2
+    outer_sem, core_sem = angles, angles + 1
 
     for copy in drift_copies:
         copy.wait()
@@ -190,21 +215,41 @@
     pl.semaphore_wait(barrier, slabs + 1)
     for copy in edge_copies(0):
         copy.start()
-    for a in range(1, AHEAD):
+    align_and_send(0, al.at[0], 0, (inner,), (inner,))
+    own_copy(0, al.at[0], inner, 0).start()
+    level_and_send(1)
+    take_edges(0)
+    align_and_send(0, al_outer, outer_sem, outer, outer)
+    for n, piece in enumerate(outer):
+        own_copy(0, al_outer, piece, angles + n).start()
+    for a in range(2, AHEAD + 1):
         level_and_send(a)
 
     def both(a, carry):
-        finish(a)
+        take_edges(a)
+        align_and_send(a, al.at[a], a, (whole,), (whole,))
+        own_copy(a, al.at[a], whole, a).start()
         level_and_send(a + AHEAD)
         return carry
 
-    lax.fori_loop(0, angles - AHEAD, both, 0)
+    lax.fori_loop(1, angles - AHEAD, both, 0)
 
     def last(a, carry):
-        finish(a)
+        take_edges(a)
+        align_and_send(a, al.at[a], a, (whole,), rims)
+        own_copy(a, al.at[a], whole, a).start()
         return carry
 
-    lax.fori_loop(angles - AHEAD, angles, last, 0)
+    lax.fori_loop(late, angles, last, 0)
+
+    def last_core(a, carry):
+        def one(n, carry):
+            rows_to(partner(n), a, al.at[a], core, core_sem + (a - late)).start()
+            return carry
+
+        return lax.fori_loop(0, slabs - 1, one, carry)
+
+    lax.fori_loop(late, angles, last_core, 0)
 
     for k in range(3):
         ramp[k] = ramp_tile(RW * (k - 1)).astype(BF16)
@@ -224,16 +269,15 @@
             ),
         )
 
-    def arrived(k):
+    def arrived(sem, width):
+        part_of = sino.at[pl.ds(0, slabs - 1), 0, :, pl.ds(0, width)]
         return pltpu.make_async_remote_copy(
-            al.at[k, pl.ds(0, slabs - 1)], sino.at[pl.ds(0, slabs - 1), k], s_sem.at[k], r_sem.at[k],
-            device_id={"ang": me}, device_id_type=MESH,
+            part_of, part_of, s_sem.at[sem], r_sem.at[sem], device_id={"ang": me}, device_id_type=MESH
         )
 
-    def collect(k, total):
-        pltpu.make_async_copy(al.at[k, me], sino.at[me, k], own_sem.at[k]).wait()
-        arrived(k).wait_recv()
-        return lax.fori_loop(0, slabs, lambda i, t: t + sino[i, k].astype(F32), total)
+    def summed(k, first, number, total):
+        lanes = pl.ds(first * LANES, number * LANES)
+        return lax.fori_loop(0, slabs, lambda i, t: t + sino[i, k, :, lanes].astype(F32), total)
 
     def pass_on(k):
         for copy in halo_copies(k):
@@ -260,18 +304,34 @@
             )
             part[:, k, :, pl.ds(n * RW, RW)] = acc.reshape(slabs, slab, RW)
 
-    total = collect(0, jnp.zeros((slab, width), F32))
+    own_copy(0, al.at[0], inner, 0).wait()
+    for n, piece in enumerate(outer):
+        own_copy(0, al_outer, piece, angles + n).wait()
+    arrived(0, inner[1] * LANES).wait_recv()
+    arrived(outer_sem, 2 * LANES).wait_recv()
     pass_on(0)
+    total = summed(0, 0, blocks, jnp.zeros((slab, width), F32))
 
     def middle(k, total):
-        total = collect(k, total)
+        own_copy(k, al.at[k], whole, k).wait()
+        arrived(k, width).wait_recv()
         pass_on(k)
+        total = summed(k, 0, blocks, total)
         filt(k - 1)
         return total
 
-    total = lax.fori_loop(1, angles - 1, middle, total)
-    total = collect(angles - 1, total)
-    mean[:, pl.ds(MEDGE, width)] = total / float(slabs * angles)
+    total = lax.fori_loop(1, late, middle, total)
+    count = float(slabs * angles)
+    sides = [total[:, first * LANES : (first + number) * LANES] for first, number in rims]
+    centre = total[:, core[0] * LANES : (core[0] + core[1]) * LANES]
+    for k in (late, late + 1):
+        own_copy(k, al.at[k], whole, k).wait()
+        arrived(k, 2 * MEDGE).wait_recv()
+        sides = [summed(k, first, number, side) for (first, number), side in zip(rims, sides)]
+        if k == late:
+            pass_on(k)
+    for (first, number), side in zip(rims, sides):
+        mean[:, pl.ds(MEDGE + first * LANES, number * LANES)] = side / count
 
     mean_copies = (
         pltpu.make_async_remote_copy(
@@ -286,15 +346,20 @@
     for copy in mean_copies:
         copy.start()
     pass_on(angles - 1)
-    filt(angles - 2)
-
-    def drain(k, carry):
-        arrived(k).wait_send()
-        for copy in edge_copies(k):
+    filt(late - 1)
+
+    for a in range(angles):
+        arrived(a, inner[1] * LANES if a == 0 else 2 * MEDGE if a >= late else width).wait_send()
+        for copy in edge_copies(a):
             copy.wait_send()
-        return carry
-
-    lax.fori_loop(0, angles, drain, 0)
+    arrived(outer_sem, 2 * LANES).wait_send()
+
+    arrived(core_sem, core[1] * LANES).wait_recv()
+    centre = summed(late, core[0], core[1], centre)
+    filt(late)
+    arrived(core_sem + 1, core[1] * LANES).wait_recv()
+    centre = summed(late + 1, core[0], core[1], centre)
+    mean[:, pl.ds(MEDGE + core[0] * LANES, core[1] * LANES)] = centre / count
     for copy in mean_copies:
         copy.wait_recv()
 
@@ -330,6 +395,8 @@
         kept[:, pl.ds(n * RW, RW)] = acc[0:slab] + acc[slab : 2 * slab] + acc[2 * slab : 3 * slab]
 
     filt(angles - 1)
+    for sem in (core_sem, core_sem + 1):
+        arrived(sem, core[1] * LANES).wait_send()
     for side, halo in ((0, halo_l), (1, halo_r)):
         pltpu.make_async_remote_copy(
             halo, halo, hs_sem.at[side], hr_sem.at[side, 0], device_id={"col": left}, device_id_type=MESH
@@ -386,6 +453,7 @@
             pltpu.VMEM((angles, 2, rows, LANES), BF16),
             pltpu.VMEM((angles, 2, rows, LANES), BF16),
             pltpu.VMEM((angles, slabs, slab, width), BF16),
+            pltpu.VMEM((slabs, slab, width), BF16),
             pltpu.VMEM((slabs, angles, slab, width), BF16),
             pltpu.VMEM((slabs, angles, slab, RW), BF16),
             pltpu.VMEM((slabs, angles, slab, RW), BF16),
@@ -398,9 +466,9 @@
             dma,
             dma((angles, 2)),
             dma((angles, 2)),
-            dma((angles,)),
-            dma((angles,)),
-            dma((angles,)),
+            dma((angles + 2,)),
+            dma((angles + 3,)),
+            dma((angles + 3,)),
             dma((2,)),
             dma((2, angles)),
             dma((2,)),

time: 67.5 us -> 65.4 us (0.969)
  Pallas kernels: 67.4 us -> 65.3 us
    pallas_call x1, Pallas kernels: 63.9 us -> 61.9 us  [on_device(): pl.pallas_call(exchange_kernel, name='exchange', out_shape=(pltpu.VMEM((s...]
where the time goes in v2:
time: 65.4 us; the launch traced here: 65.3 us
  Pallas kernels  65.3 us (100%)
    pallas_call x1, Pallas kernels, on_device(): pl.pallas_call(exchange_kernel, name='exchange', out_shape=(pltpu.VMEM((s...  61.9 us
    pallas_call x1, Pallas kernels, on_device(): pl.pallas_call(subtract_kernel, name='subtract', out_shape=jax.ShapeDtype...  3.45 us

profile of v2, /device:TPU:0, one launch (start us, length us, event | category | flops | bytes accessed | tf_op | source)
XLA Modules:
  0.0 65.3 jit_solution(14650385566155173210)
XLA Ops:
  0.0 61.9 %exchange.1 = (f32[16,8,16,1024]{3,2,1,0:T(8,128)S(1)}, f32[16,1024]{1,0:T(8,128)S(1)}) custom-call(bf16[8,256,1024]{2,1,0:T(8,128)(2,1)} %proj.1, f32[256,1024]{1,0:T(8,128)} %offset.1, s32[2,128]{1,0:T(2,128)} %doff_in.1, s32[2,128]{1,0:T(2,128)} %dfrac_in.1, s32[16]{0:T(128)} %widths_in.1), custom_call_target="tpu_custom_call" | custom-call | tf_op jit(solution)/shard_map/exchange/pallas_call | solution.py:436
  61.9 3.5 %subtract.1 = f32[16,8,16,1024]{3,2,1,0:T(8,128)} custom-call(f32[16,8,16,1024]{3,2,1,0:T(8,128)S(1)} %get-tuple-element.7.part, f32[16,1024]{1,0:T(8,128)S(1)} %get-tuple-element.8.kept), custom_call_target="tpu_custom_call" | custom-call | tf_op jit(solution)/shard_map/subtract/pallas_call | solution.py:481

commit v3 on v2

--- a/solution.py
+++ b/solution.py
@@ -14,8 +14,7 @@
 F32 = jnp.float32
 BF16 = jnp.bfloat16
 
-ORDER = (10, 6, 11, 14, 9, 2, 8, 5, 15, 7, 13, 1, 4, 3, 12, 0)
-DIGITS = 7
+ORDER = (10, 6, 11, 14, 9, 2, 8, 5, 15, 7, 13, 1, 4, 3, 12)
 SIDE = 4
 MARGIN = 8
 LANES = 128
@@ -48,7 +47,7 @@
 def exchange_kernel(
     proj, offset, doff_in, dfrac_in, widths_in,
     part, kept,
-    pbuf, obuf, doff, dfrac, widths, padded, lev, sent, got, al, al_outer, sino, halo_l, halo_r, mean, cyc, ramp, ends,
+    pbuf, obuf, doff, dfrac, widths, padded, lev, bands, al, al_outer, sino, halo_l, halo_r, mean, cyc, ramp, ends,
     d_sem, p_sem, o_sem, es_sem, er_sem, own_sem, s_sem, r_sem, hs_sem, hr_sem, ms_sem, mr_sem,
 ):
     me = lax.axis_index("ang")
@@ -62,19 +61,12 @@
     left = lax.rem(col + n_col - 1, n_col)
     right = lax.rem(col + 1, n_col)
 
-    def partner(n):
-        if isinstance(n, int):
-            place = ORDER[n]
-        else:
-            place = 0
-            for first in range(0, slabs, DIGITS):
-                code = sum(p << (4 * d) for d, p in enumerate(ORDER[first : first + DIGITS]))
-                here = jnp.clip(n - first, 0, DIGITS - 1)
-                digit = lax.shift_right_logical(jnp.int32(code), 4 * here) & 15
-                place = jnp.where(n >= first, digit, place)
+    def partner(place):
         return lax.rem(y + SIDE + sign * (place // SIDE), SIDE) * SIDE + lax.rem(
-            x + SIDE + sign * lax.rem(place, SIDE), SIDE
+            x + SIDE + sign * (place % SIDE), SIDE
         )
+
+    partners = [partner(place) for place in ORDER]
 
     def frame_copy(a):
         return pltpu.make_async_copy(proj.at[a], pbuf.at[a], p_sem.at[a])
@@ -93,8 +85,8 @@
         frame_copy(a).start()
 
     barrier = pltpu.get_barrier_semaphore()
-    for n in range(slabs - 1):
-        pl.semaphore_signal(barrier, 1, device_id={"ang": partner(n)}, device_id_type=MESH)
+    for to in partners:
+        pl.semaphore_signal(barrier, 1, device_id={"ang": to}, device_id_type=MESH)
     for neighbour in (left, right):
         pl.semaphore_signal(barrier, 1, device_id={"col": neighbour}, device_id_type=MESH)
 
@@ -105,12 +97,12 @@
     def edge_copies(a):
         return (
             pltpu.make_async_remote_copy(
-                sent.at[a, 1], got.at[a, 0], es_sem.at[a, 0], er_sem.at[a, 0],
-                device_id={"col": right}, device_id_type=MESH,
+                lev.at[a, :, pl.ds(width, LANES)], lev.at[a, :, pl.ds(0, LANES)],
+                es_sem.at[a, 0], er_sem.at[a, 0], device_id={"col": right}, device_id_type=MESH,
             ),
             pltpu.make_async_remote_copy(
-                sent.at[a, 0], got.at[a, 1], es_sem.at[a, 1], er_sem.at[a, 1],
-                device_id={"col": left}, device_id_type=MESH,
+                lev.at[a, :, pl.ds(LANES, LANES)], lev.at[a, :, pl.ds(LANES + width, LANES)],
+                es_sem.at[a, 1], er_sem.at[a, 1], device_id={"col": left}, device_id_type=MESH,
             ),
         )
 
@@ -137,9 +129,8 @@
             for k in range(1, 4):
                 total = total + taps[k] * padded[:, pl.ds(base + k, slab), :]
             total = total.astype(BF16)
-            sent[a, 0, pl.ds(at, slab), :] = total[0]
-            sent[a, 1, pl.ds(at, slab), :] = total[blocks - 1]
-            lev[lax.rem(a, AHEAD + 1), pl.ds(1, blocks), pl.ds(at, slab), :] = total.astype(F32)
+            for b in range(blocks):
+                lev[a, pl.ds(at, slab), pl.ds((b + 1) * LANES, LANES)] = total[b]
             return carry
 
         lax.fori_loop(0, slabs, mix, 0)
@@ -151,37 +142,40 @@
             device_id={"ang": to}, device_id_type=MESH,
         )
 
-    def align_and_send(a, buf, sem, made, gone):
+    def weights(a):
         shift = doff[1, me * angles + a]
         taps = cubic_taps(dfrac[1, me * angles + a])
-        slot = lax.rem(a, AHEAD + 1)
-        lane = lax.broadcasted_iota(jnp.int32, (1, slab, LANES), 2)
-
-        def mix(n, carry):
-            j = partner(n)
-            at = pl.multiple_of(j * slab, slab)
-            for first, number in made:
-                total = None
-                for k in range(4):
-                    moved = shift + (k - 1)
-                    back = jnp.where(moved < 0, 1, 0)
-                    turn = moved + back * LANES
-                    block = lev[slot, pl.ds(first + 1 - back, number + 1), pl.ds(at, slab), :]
-                    rolled = pltpu.roll(block, lax.rem(LANES - turn, LANES), 2)
-                    piece = taps[k] * jnp.where(lane < LANES - turn, rolled[0:number], rolled[1 : number + 1])
-                    total = piece if total is None else total + piece
-                out = total.astype(BF16)
-                for b in range(number):
-                    buf[j, :, pl.ds((first + b) * LANES, LANES)] = out[b]
-
-            @pl.when(n > 0)
-            def _():
-                for piece in gone:
-                    rows_to(partner(n - 1), a, buf, piece, sem).start()
-
+        slot = lax.rem(a, 2)
+        step = 64
+
+        def build(i, carry):
+            at = pl.multiple_of(i * step, step)
+            index = lax.broadcasted_iota(jnp.int32, (step, RW), 0) - lax.broadcasted_iota(jnp.int32, (step, RW), 1)
+            index = index + (at - LANES - shift + 1)
+            value = jnp.zeros((step, RW), F32)
+            for k in range(4):
+                value = jnp.where(index == k, taps[k], value)
+            for p in range(3):
+                piece = value.astype(BF16)
+                bands[slot, p, pl.ds(at, step), :] = piece
+                value = value - piece.astype(F32)
             return carry
 
-        lax.fori_loop(0, slabs, mix, 0)
+        lax.fori_loop(0, 2 * RW // step, build, 0)
+
+    def align(a, buf, made):
+        slot = lax.rem(a, 2)
+        for n in made:
+            window = lev[a, :, pl.ds(n * RW, 2 * RW)]
+            total = jnp.dot(window, bands[slot, 2], preferred_element_type=F32)
+            total = total + jnp.dot(window, bands[slot, 1], preferred_element_type=F32)
+            total = total + jnp.dot(window, bands[slot, 0], preferred_element_type=F32)
+            buf[:, :, pl.ds(n * RW, RW)] = total.astype(BF16).reshape(slabs, slab, RW)
+
+    def send(a, buf, sem, gone):
+        for to in partners:
+            for piece in gone:
+                rows_to(to, a, buf, piece, sem).start()
 
     def own_copy(a, buf, piece, sem):
         lanes = pl.ds(piece[0] * LANES, piece[1] * LANES)
@@ -195,13 +189,15 @@
     def take_edges(a):
         for copy in edge_copies(a):
             copy.wait_recv()
-        slot = lax.rem(a, AHEAD + 1)
-        lev[slot, 0] = jnp.where(col > 0, got[a, 0].astype(F32), 0.0)
-        lev[slot, blocks + 1] = jnp.where(col < n_col - 1, got[a, 1].astype(F32), 0.0)
+        before, after = pl.ds(0, LANES), pl.ds(LANES + width, LANES)
+        lev[a, :, before] = jnp.where(col > 0, lev[a, :, before].astype(F32), 0.0).astype(BF16)
+        lev[a, :, after] = jnp.where(col < n_col - 1, lev[a, :, after].astype(F32), 0.0).astype(BF16)
 
     whole = (0, blocks)
-    inner = (1, blocks - 2)
-    outer = ((0, 1), (blocks - 1, 1))
+    step = RW // LANES
+    inner = (step, blocks - 2 * step)
+    outer = ((0, step), (blocks - step, step))
+    parts = width // RW
     rim = MEDGE // LANES
     rims = ((0, rim), (blocks - rim, rim))
     core = (rim, blocks - 2 * rim)
@@ -210,24 +206,29 @@
 
     for copy in drift_copies:
         copy.wait()
+    weights(0)
     offset_copy.wait()
     level(0)
     pl.semaphore_wait(barrier, slabs + 1)
     for copy in edge_copies(0):
         copy.start()
-    align_and_send(0, al.at[0], 0, (inner,), (inner,))
+    align(0, al.at[0], range(1, parts - 1))
+    weights(1)
+    send(0, al.at[0], 0, (inner,))
     own_copy(0, al.at[0], inner, 0).start()
     level_and_send(1)
     take_edges(0)
-    align_and_send(0, al_outer, outer_sem, outer, outer)
+    align(0, al_outer, (0, parts - 1))
+    level_and_send(2)
+    send(0, al_outer, outer_sem, outer)
     for n, piece in enumerate(outer):
         own_copy(0, al_outer, piece, angles + n).start()
-    for a in range(2, AHEAD + 1):
-        level_and_send(a)
 
     def both(a, carry):
         take_edges(a)
-        align_and_send(a, al.at[a], a, (whole,), (whole,))
+        align(a, al.at[a], range(parts))
+        weights(a + 1)
+        send(a, al.at[a], a, (whole,))
         own_copy(a, al.at[a], whole, a).start()
         level_and_send(a + AHEAD)
         return carry
@@ -236,18 +237,17 @@
 
     def last(a, carry):
         take_edges(a)
-        align_and_send(a, al.at[a], a, (whole,), rims)
+        align(a, al.at[a], range(parts))
+        weights(jnp.minimum(a + 1, angles - 1))
+        send(a, al.at[a], a, rims)
         own_copy(a, al.at[a], whole, a).start()
         return carry
 
     lax.fori_loop(late, angles, last, 0)
 
     def last_core(a, carry):
-        def one(n, carry):
-            rows_to(partner(n), a, al.at[a], core, core_sem + (a - late)).start()
-            return carry
-
-        return lax.fori_loop(0, slabs - 1, one, carry)
+        send(a, al.at[a], core_sem + (a - late), (core,))
+        return carry
 
     lax.fori_loop(late, angles, last_core, 0)
 
@@ -283,8 +283,6 @@
         for copy in halo_copies(k):
             copy.start()
 
-    parts = width // RW
-
     def filt(k):
         for copy in halo_copies(k):
             copy.wait_recv()
@@ -308,7 +306,7 @@
     for n, piece in enumerate(outer):
         own_copy(0, al_outer, piece, angles + n).wait()
     arrived(0, inner[1] * LANES).wait_recv()
-    arrived(outer_sem, 2 * LANES).wait_recv()
+    arrived(outer_sem, 2 * RW).wait_recv()
     pass_on(0)
     total = summed(0, 0, blocks, jnp.zeros((slab, width), F32))
 
@@ -352,7 +350,7 @@
         arrived(a, inner[1] * LANES if a == 0 else 2 * MEDGE if a >= late else width).wait_send()
         for copy in edge_copies(a):
             copy.wait_send()
-    arrived(outer_sem, 2 * LANES).wait_send()
+    arrived(outer_sem, 2 * RW).wait_send()
 
     arrived(core_sem, core[1] * LANES).wait_recv()
     centre = summed(late, core[0], core[1], centre)
@@ -449,9 +447,8 @@
             pltpu.SMEM(drift_offsets.shape, jnp.int32),
             pltpu.SMEM(cycle_widths.shape, jnp.int32),
             pltpu.VMEM((blocks, rows + 2 * MARGIN, LANES), F32),
-            pltpu.VMEM((AHEAD + 1, blocks + 2, rows, LANES), F32),
-            pltpu.VMEM((angles, 2, rows, LANES), BF16),
-            pltpu.VMEM((angles, 2, rows, LANES), BF16),
+            pltpu.VMEM((angles, rows, width + 2 * LANES), BF16),
+            pltpu.VMEM((2, 3, 2 * RW, RW), BF16),
             pltpu.VMEM((angles, slabs, slab, width), BF16),
             pltpu.VMEM((slabs, slab, width), BF16),
             pltpu.VMEM((slabs, angles, slab, width), BF16),

time: 65.4 us -> 63.1 us (0.965)
  Pallas kernels: 65.3 us -> 63 us
    pallas_call x1, Pallas kernels: 61.9 us -> 59.6 us  [on_device(): pl.pallas_call(exchange_kernel, name='exchange', out_shape=(pltpu.VMEM((s...]
where the time goes in v3:
time: 63.1 us; the launch traced here: 63 us
  Pallas kernels  63 us (100%)
    pallas_call x1, Pallas kernels, on_device(): pl.pallas_call(exchange_kernel, name='exchange', out_shape=(pltpu.VMEM((s...  59.6 us
    pallas_call x1, Pallas kernels, on_device(): pl.pallas_call(subtract_kernel, name='subtract', out_shape=jax.ShapeDtype...  3.45 us

profile of v3, /device:TPU:0, one launch (start us, length us, event | category | flops | bytes accessed | tf_op | source)
XLA Modules:
  0.0 63.0 jit_solution(656801918460619870)
XLA Ops:
  0.0 59.6 %exchange.1 = (f32[16,8,16,1024]{3,2,1,0:T(8,128)S(1)}, f32[16,1024]{1,0:T(8,128)S(1)}) custom-call(bf16[8,256,1024]{2,1,0:T(8,128)(2,1)} %proj.1, f32[256,1024]{1,0:T(8,128)} %offset.1, s32[2,128]{1,0:T(2,128)} %doff_in.1, s32[2,128]{1,0:T(2,128)} %dfrac_in.1, s32[16]{0:T(128)} %widths_in.1), custom_call_target="tpu_custom_call" | custom-call | tf_op jit(solution)/shard_map/exchange/pallas_call | solution.py:434
  59.6 3.5 %subtract.1 = f32[16,8,16,1024]{3,2,1,0:T(8,128)} custom-call(f32[16,8,16,1024]{3,2,1,0:T(8,128)S(1)} %get-tuple-element.7.part, f32[16,1024]{1,0:T(8,128)S(1)} %get-tuple-element.8.kept), custom_call_target="tpu_custom_call" | custom-call | tf_op jit(solution)/shard_map/subtract/pallas_call | solution.py:478

commit v4 on v3

--- a/solution.py
+++ b/solution.py
@@ -18,6 +18,7 @@
 SIDE = 4
 MARGIN = 8
 LANES = 128
+LATE = 3
 AHEAD = 2
 MEDGE = 384
 
@@ -81,8 +82,7 @@
     offset_copy = pltpu.make_async_copy(offset, obuf, o_sem)
     frame_copy(0).start()
     offset_copy.start()
-    for a in range(1, angles):
-        frame_copy(a).start()
+    frame_copy(1).start()
 
     barrier = pltpu.get_barrier_semaphore()
     for to in partners:
@@ -201,7 +201,7 @@
     rim = MEDGE // LANES
     rims = ((0, rim), (blocks - rim, rim))
     core = (rim, blocks - 2 * rim)
-    late = angles - 2
+    late = angles - LATE
     outer_sem, core_sem = angles, angles + 1
 
     for copy in drift_copies:
@@ -209,14 +209,16 @@
     weights(0)
     offset_copy.wait()
     level(0)
+    for a in range(2, angles):
+        frame_copy(a).start()
+    align(0, al.at[0], range(1, parts - 1))
     pl.semaphore_wait(barrier, slabs + 1)
     for copy in edge_copies(0):
         copy.start()
-    align(0, al.at[0], range(1, parts - 1))
-    weights(1)
     send(0, al.at[0], 0, (inner,))
     own_copy(0, al.at[0], inner, 0).start()
     level_and_send(1)
+    weights(1)
     take_edges(0)
     align(0, al_outer, (0, parts - 1))
     level_and_send(2)
@@ -233,17 +235,17 @@
         level_and_send(a + AHEAD)
         return carry
 
-    lax.fori_loop(1, angles - AHEAD, both, 0)
-
-    def last(a, carry):
+    lax.fori_loop(1, late, both, 0)
+
+    for a in range(late, angles):
         take_edges(a)
         align(a, al.at[a], range(parts))
-        weights(jnp.minimum(a + 1, angles - 1))
+        if a + 1 < angles:
+            weights(a + 1)
         send(a, al.at[a], a, rims)
         own_copy(a, al.at[a], whole, a).start()
-        return carry
-
-    lax.fori_loop(late, angles, last, 0)
+        if a + AHEAD < angles:
+            level_and_send(a + AHEAD)
 
     def last_core(a, carry):
         send(a, al.at[a], core_sem + (a - late), (core,))
@@ -286,7 +288,9 @@
     def filt(k):
         for copy in halo_copies(k):
             copy.wait_recv()
-
+        filt_here(k)
+
+    def filt_here(k):
         def window(m):
             if m < 0:
                 return halo_l[:, k].reshape(rows, RW)
@@ -322,11 +326,11 @@
     count = float(slabs * angles)
     sides = [total[:, first * LANES : (first + number) * LANES] for first, number in rims]
     centre = total[:, core[0] * LANES : (core[0] + core[1]) * LANES]
-    for k in (late, late + 1):
+    for k in range(late, angles):
         own_copy(k, al.at[k], whole, k).wait()
         arrived(k, 2 * MEDGE).wait_recv()
         sides = [summed(k, first, number, side) for (first, number), side in zip(rims, sides)]
-        if k == late:
+        if k < angles - 1:
             pass_on(k)
     for (first, number), side in zip(rims, sides):
         mean[:, pl.ds(MEDGE + first * LANES, number * LANES)] = side / count
@@ -352,38 +356,48 @@
             copy.wait_send()
     arrived(outer_sem, 2 * RW).wait_send()
 
-    arrived(core_sem, core[1] * LANES).wait_recv()
-    centre = summed(late, core[0], core[1], centre)
-    filt(late)
-    arrived(core_sem + 1, core[1] * LANES).wait_recv()
-    centre = summed(late + 1, core[0], core[1], centre)
-    mean[:, pl.ds(MEDGE + core[0] * LANES, core[1] * LANES)] = centre / count
+    for n in range(LATE - 1):
+        arrived(core_sem + n, core[1] * LANES).wait_recv()
+        centre = summed(late + n, core[0], core[1], centre)
+        filt(late + n)
     for copy in mean_copies:
         copy.wait_recv()
 
     total_cols = n_col * width
-    span = width + 2 * MEDGE
-    at = lax.broadcasted_iota(jnp.int32, (slab, span), 1) + (col * width - MEDGE)
-    inside = (at >= 0) & (at < total_cols)
     line = lax.broadcasted_iota(jnp.int32, (slab, 1), 0)
     half = jnp.zeros((slab, 1), jnp.int32)
     for r in range(slab):
         half = jnp.where(line == r, widths[r], half)
-    centre = jnp.where(inside, mean[...], 0.0)
-    running = centre
-    for j in range(1, BWMAX + 1):
-        pair = pltpu.roll(centre, j, 1) + pltpu.roll(centre, span - j, 1)
-        running = running + jnp.where(half >= j, pair, 0.0)
-    count = jnp.minimum(at, half) + jnp.minimum(total_cols - 1 - at, half) + 1
-    count = jnp.maximum(count, 1).astype(F32)
-    cycle = jnp.where(inside, centre - running / count, 0.0)
-    first = cycle.astype(BF16)
-    rest = cycle - first.astype(F32)
-    second = rest.astype(BF16)
-    third = (rest - second.astype(F32)).astype(BF16)
-    cyc[0:slab] = first
-    cyc[slab : 2 * slab] = second
-    cyc[2 * slab : 3 * slab] = third
+
+    def find_cycle(first, end):
+        start, stop = max(first - LANES, 0), min(end + LANES, width + 2 * MEDGE)
+        span = stop - start
+        at = lax.broadcasted_iota(jnp.int32, (slab, span), 1) + (col * width - MEDGE + start)
+        inside = (at >= 0) & (at < total_cols)
+        centre = jnp.where(inside, mean[:, pl.ds(start, span)], 0.0)
+        running = centre
+        for j in range(1, BWMAX + 1):
+            pair = pltpu.roll(centre, j, 1) + pltpu.roll(centre, span - j, 1)
+            running = running + jnp.where(half >= j, pair, 0.0)
+        terms = jnp.minimum(at, half) + jnp.minimum(total_cols - 1 - at, half) + 1
+        terms = jnp.maximum(terms, 1).astype(F32)
+        rest = jnp.where(inside, centre - running / terms, 0.0)[:, first - start : end - start]
+        for p in range(3):
+            piece = rest.astype(BF16)
+            cyc[p * slab : (p + 1) * slab, pl.ds(first, end - first)] = piece
+            rest = rest - piece.astype(F32)
+
+    inner_first = MEDGE + (core[0] - 1) * LANES
+    inner_end = MEDGE + (core[0] + core[1] + 1) * LANES
+    find_cycle(0, inner_first)
+    find_cycle(inner_end, width + 2 * MEDGE)
+    arrived(core_sem + LATE - 1, core[1] * LANES).wait_recv()
+    for copy in halo_copies(angles - 1):
+        copy.wait_recv()
+    centre = summed(angles - 1, core[0], core[1], centre)
+    mean[:, pl.ds(MEDGE + core[0] * LANES, core[1] * LANES)] = centre / count
+    filt_here(angles - 1)
+    find_cycle(inner_first, inner_end)
     for n in range(parts):
         acc = jnp.zeros((3 * slab, RW), F32)
         for k in range(3):
@@ -392,8 +406,7 @@
             )
         kept[:, pl.ds(n * RW, RW)] = acc[0:slab] + acc[slab : 2 * slab] + acc[2 * slab : 3 * slab]
 
-    filt(angles - 1)
-    for sem in (core_sem, core_sem + 1):
+    for sem in range(core_sem, core_sem + LATE):
         arrived(sem, core[1] * LANES).wait_send()
     for side, halo in ((0, halo_l), (1, halo_r)):
         pltpu.make_async_remote_copy(
@@ -404,13 +417,16 @@
 
 
 def subtract_kernel(part, kept, out, obuf, o_sem):
-    slabs = part.shape[0]
+    steps = o_sem.shape[0]
+    group = part.shape[0] // steps
 
     def put(i):
-        return pltpu.make_async_copy(obuf.at[i], out.at[i], o_sem.at[i])
+        some = pl.ds(i * group, group)
+        return pltpu.make_async_copy(obuf.at[some], out.at[some], o_sem.at[i])
 
     def step(i, carry):
-        obuf[i] = part[i] - kept[...]
+        some = pl.ds(i * group, group)
+        obuf[some] = part[some] - kept[...]
         put(i).start()
         return carry
 
@@ -418,8 +434,8 @@
         put(i).wait()
         return carry
 
-    lax.fori_loop(0, slabs, step, 0)
-    lax.fori_loop(0, slabs, wait, 0)
+    lax.fori_loop(0, steps, step, 0)
+    lax.fori_loop(0, steps, wait, 0)
 
 
 def on_device(projections, detector_offset, drift_offsets, drift_fractions, cycle_widths):
@@ -464,8 +480,8 @@
             dma((angles, 2)),
             dma((angles, 2)),
             dma((angles + 2,)),
-            dma((angles + 3,)),
-            dma((angles + 3,)),
+            dma((angles + 1 + LATE,)),
+            dma((angles + 1 + LATE,)),
             dma((2,)),
             dma((2, angles)),
             dma((2,)),
@@ -475,16 +491,16 @@
             collective_id=0, has_side_effects=True, vmem_limit_bytes=54 * 1024 * 1024
         ),
     )(*(pltpu.with_memory_space_constraint(a, pltpu.HBM) for a in given))
-    filtered = pl.pallas_call(
+    frames = (slabs * angles, slab, width)
+    return pl.pallas_call(
         subtract_kernel,
         name="subtract",
-        out_shape=jax.ShapeDtypeStruct((slabs, angles, slab, width), F32),
+        out_shape=jax.ShapeDtypeStruct(frames, F32),
         in_specs=[vmem] * 2,
         out_specs=hbm,
-        scratch_shapes=[pltpu.VMEM((slabs, angles, slab, width), F32), dma((slabs,))],
+        scratch_shapes=[pltpu.VMEM(frames, F32), dma((slabs,))],
         compiler_params=pltpu.CompilerParams(vmem_limit_bytes=24 * 1024 * 1024),
-    )(part, kept)
-    return filtered.reshape(slabs * angles, slab, width)
+    )(part.reshape(frames), kept)
 
 
 def solution(mesh):

time: 63.1 us -> 62.5 us (level)
  no operation moved by 1% of the time
where the time goes in v4:
time: 62.5 us; the launch traced here: 62.4 us
  Pallas kernels  62.4 us (100%)
    pallas_call x1, Pallas kernels, on_device(): pl.pallas_call(exchange_kernel, name='exchange', out_shape=(pltpu.VMEM((s...  58.9 us
    pallas_call x1, Pallas kernels, on_device(): pl.pallas_call(subtract_kernel, name='subtract', out_shape=jax.ShapeDtype...  3.45 us

profile of v4, /device:TPU:0, one launch (start us, length us, event | category | flops | bytes accessed | tf_op | source)
XLA Modules:
  0.0 62.4 jit_solution(14119889251177442153)
XLA Ops:
  0.0 58.9 %exchange.1 = (f32[16,8,16,1024]{3,2,1,0:T(8,128)S(1)}, f32[16,1024]{1,0:T(8,128)S(1)}) custom-call(bf16[8,256,1024]{2,1,0:T(8,128)(2,1)} %proj.1, f32[256,1024]{1,0:T(8,128)} %offset.1, s32[2,128]{1,0:T(2,128)} %doff_in.1, s32[2,128]{1,0:T(2,128)} %dfrac_in.1, s32[16]{0:T(128)} %widths_in.1), custom_call_target="tpu_custom_call" | custom-call | tf_op jit(solution)/shard_map/exchange/pallas_call | solution.py:450
  58.9 3.5 %subtract.1 = f32[128,16,1024]{2,1,0:T(8,128)} custom-call(f32[128,16,1024]{2,1,0:T(8,128)S(1)} %bitcast.1, f32[16,1024]{1,0:T(8,128)S(1)} %get-tuple-element.8.kept), custom_call_target="tpu_custom_call" | custom-call | tf_op jit(solution)/shard_map/subtract/pallas_call | solution.py:495

commit v5 on v4

--- a/solution.py
+++ b/solution.py
@@ -288,9 +288,9 @@
     def filt(k):
         for copy in halo_copies(k):
             copy.wait_recv()
-        filt_here(k)
-
-    def filt_here(k):
+        filt_here(k, range(-1, parts + 1), False)
+
+    def filt_here(k, windows, add):
         def window(m):
             if m < 0:
                 return halo_l[:, k].reshape(rows, RW)
@@ -299,12 +299,16 @@
             return sino[:, k, :, pl.ds(m * RW, RW)].reshape(rows, RW)
 
         for n in range(parts):
-            acc = jnp.dot(window(n), ramp[1], preferred_element_type=F32)
-            acc = acc + jnp.dot(window(n - 1), ends[0] if n == 0 else ramp[0], preferred_element_type=F32)
-            acc = acc + jnp.dot(
-                window(n + 1), ends[1] if n == parts - 1 else ramp[2], preferred_element_type=F32
-            )
-            part[:, k, :, pl.ds(n * RW, RW)] = acc.reshape(slabs, slab, RW)
+            acc = None
+            for m in (n, n - 1, n + 1):
+                if m not in windows:
+                    continue
+                taps = ends[0] if m < 0 else ends[1] if m == parts else ramp[m - n + 1]
+                term = jnp.dot(window(m), taps, preferred_element_type=F32)
+                acc = term if acc is None else acc + term
+            lanes = pl.ds(n * RW, RW)
+            acc = acc.reshape(slabs, slab, RW)
+            part[:, k, :, lanes] = part[:, k, :, lanes] + acc if add else acc
 
     own_copy(0, al.at[0], inner, 0).wait()
     for n, piece in enumerate(outer):
@@ -391,12 +395,13 @@
     inner_end = MEDGE + (core[0] + core[1] + 1) * LANES
     find_cycle(0, inner_first)
     find_cycle(inner_end, width + 2 * MEDGE)
-    arrived(core_sem + LATE - 1, core[1] * LANES).wait_recv()
     for copy in halo_copies(angles - 1):
         copy.wait_recv()
+    filt_here(angles - 1, (-1, 0, parts - 1, parts), False)
+    arrived(core_sem + LATE - 1, core[1] * LANES).wait_recv()
     centre = summed(angles - 1, core[0], core[1], centre)
     mean[:, pl.ds(MEDGE + core[0] * LANES, core[1] * LANES)] = centre / count
-    filt_here(angles - 1)
+    filt_here(angles - 1, range(1, parts - 1), True)
     find_cycle(inner_first, inner_end)
     for n in range(parts):
         acc = jnp.zeros((3 * slab, RW), F32)

time: 62.5 us -> 62.7 us (level)
  no operation moved by 1% of the time
where the time goes in v5:
time: 62.7 us; the launch traced here: 62.6 us
  Pallas kernels  62.6 us (100%)
    pallas_call x1, Pallas kernels, on_device(): pl.pallas_call(exchange_kernel, name='exchange', out_shape=(pltpu.VMEM((s...  59.2 us
    pallas_call x1, Pallas kernels, on_device(): pl.pallas_call(subtract_kernel, name='subtract', out_shape=jax.ShapeDtype...  3.45 us

profile of v5, /device:TPU:0, one launch (start us, length us, event | category | flops | bytes accessed | tf_op | source)
XLA Modules:
  0.0 62.6 jit_solution(1159553486613166366)
XLA Ops:
  0.0 59.2 %exchange.1 = (f32[16,8,16,1024]{3,2,1,0:T(8,128)S(1)}, f32[16,1024]{1,0:T(8,128)S(1)}) custom-call(bf16[8,256,1024]{2,1,0:T(8,128)(2,1)} %proj.1, f32[256,1024]{1,0:T(8,128)} %offset.1, s32[2,128]{1,0:T(2,128)} %doff_in.1, s32[2,128]{1,0:T(2,128)} %dfrac_in.1, s32[16]{0:T(128)} %widths_in.1), custom_call_target="tpu_custom_call" | custom-call | tf_op jit(solution)/shard_map/exchange/pallas_call | solution.py:455
  59.2 3.5 %subtract.1 = f32[128,16,1024]{2,1,0:T(8,128)} custom-call(f32[128,16,1024]{2,1,0:T(8,128)S(1)} %bitcast.1, f32[16,1024]{1,0:T(8,128)S(1)} %get-tuple-element.8.kept), custom_call_target="tpu_custom_call" | custom-call | tf_op jit(solution)/shard_map/subtract/pallas_call | solution.py:500
